TPU v7x, 32 devices: a whole 2x2x4 slice. The times are simulated.
32 devices in a mesh: dp: 16 (over z, y, x), rep: 2 (over core).
Axes of the slice: x: 2, y: 2, z: 4, core: 2. Of those that a mesh axis runs over, the one named last changes fastest.
Arguments:
- hidden_old: bfloat16 [8192, 6144], P(('dp', 'rep')), may hold values from -400 to 400
- cotangent: bfloat16 [8192, 128], P(('dp', 'rep')), may hold values from -0.15625 to 0.15625
- gain_old: float32 [6144], replicated, may hold values from 0.1 to 1.9
- old_bounds: int32 [17], replicated, may hold values from 0 to 6144, as said below
- new_bounds: int32 [17], replicated, may hold values from 0 to 8192, as said below
- source_map: int32 [8192], replicated, may hold values from 0 to 6143, as said below
- weight_old: bfloat16 [8192, 128], P('dp'), may hold values from -0.078125 to 0.078125
- moment_first: float32 [8192, 128], P('dp'), may hold values from -6 to 6
- moment_second: float32 [8192, 128], P('dp'), may hold values from 0.25 to 4
Outputs:
- projected: bfloat16 [8192, 128], P(('dp', 'rep'))
- gain_grad: float32 [8192], replicated
- first_next: float32 [10240, 128], P('dp')
- second_next: float32 [10240, 128], P('dp')
- adam_step: float32 [10240, 128], P('dp')
Inputs may be any that keep to these rules, and one draw needn't show every extreme that they name: old_bounds[0] = 0, old_bounds[16] = 6144; device p holds old units old_bounds[p] to old_bounds[p+1] - 1, between 256 and 512 of them, exactly 512 on some device. new_bounds[0] = 0, new_bounds[16] = 8192; device q holds new units new_bounds[q] to new_bounds[q+1] - 1, between 384 and 640 of them, exactly 640 on some device. `source_map`: the s-th new unit of a device (counted from its first) copies an old unit held by old device (s + c) mod 16, with an offset c of that new device; so at most 40 new units of one device copy units of one old device, and some pair of devices reaches 40.
All inputs are finite; a program needn't handle non-finite values.
Results may differ from a plain program's by a relative error of at most 0.0049.
Values may be sent and summed in bfloat16 or wider, within the bound.
No kernel may reach another device: no remote copies, remote signals or barrier semaphores. Data moves between devices by JAX's collectives and lax.ppermute only.
A program may use at most 64 MiB of HBM per device.

v0:
```python
import jax
import jax.numpy as jnp
from jax import lax
from jax.sharding import PartitionSpec as P

D_OLD = 6144
D_NEW = 8192


def owners(bounds, unit_ids):
    return jnp.sum((bounds[None, 1:] <= unit_ids[:, None]).astype(jnp.int32), axis=1)


def routing(
    owner_of,
    local_of,
    table_rows,
    slot_cap,
    dev_index,
    dest_owner,
    new_bounds,
    positions,
    wanted,
    own_slots,
    dp_count,
):
    from_me = (owner_of == dev_index).astype(jnp.int32)
    before = jnp.cumsum(from_me) - from_me
    send_slot = before - before[new_bounds[dest_owner]]
    target = jnp.where(from_me > 0, dest_owner * slot_cap + send_slot, dp_count * slot_cap)
    chosen = jnp.zeros((dp_count * slot_cap,), jnp.int32).at[target].set(positions, mode="drop")
    filled = jnp.zeros((dp_count * slot_cap,), jnp.bool_).at[target].set(True, mode="drop")
    local_row = jnp.clip(local_of[chosen], 0, table_rows - 1)
    anchor = owner_of[wanted]
    earlier = (own_slots[None, :] < own_slots[:, None]) & (anchor[None, :] == anchor[:, None])
    arrival_rank = jnp.sum(earlier.astype(jnp.int32), axis=1)
    incoming = jnp.minimum(anchor * slot_cap + arrival_rank, dp_count * slot_cap - 1)
    return (local_row, filled, incoming)


def outgoing(source_table, route_info):
    return jnp.where(
        route_info[1][:, None], source_table[route_info[0]], jnp.zeros((), source_table.dtype)
    )


def arrived(source_table, route_info, live_new):
    return jnp.where(live_new[:, None], source_table[route_info[2]], 0.0)


def on_device(
    hidden_old,
    cotangent,
    gain_old,
    old_bounds,
    new_bounds,
    source_map,
    weight_old,
    moment_first,
    moment_second,
):
    dp_count = lax.axis_size("dp")
    dev_index = lax.axis_index("dp")
    old_cap = weight_old.shape[0]
    new_mean = D_NEW // dp_count
    new_cap = new_mean + new_mean // 4
    pair_cap = (new_cap + dp_count - 1) // dp_count
    positions = jnp.arange(D_NEW, dtype=jnp.int32)
    first_use = jnp.full((D_OLD,), D_NEW, jnp.int32).at[source_map].min(positions)
    unit_used = first_use < D_NEW
    keep_mask = first_use[source_map] == positions
    copies = jnp.zeros((D_OLD,), jnp.float32).at[source_map].add(1.0)
    padded = jnp.arange(dp_count * old_cap, dtype=jnp.int32)
    slot_owner = padded // old_cap
    within = padded - slot_owner * old_cap
    live_old = within < old_bounds[slot_owner + 1] - old_bounds[slot_owner]
    slot_unit = jnp.minimum(old_bounds[slot_owner] + within, D_OLD - 1)
    weight_live = live_old & unit_used[slot_unit]
    source_owner = owners(old_bounds, source_map)
    source_slot = source_owner * old_cap + source_map - old_bounds[source_owner]
    dest_owner = owners(new_bounds, positions)
    own_slots = jnp.arange(new_cap, dtype=jnp.int32)
    live_new = own_slots < new_bounds[dev_index + 1] - new_bounds[dev_index]
    wanted = jnp.minimum(new_bounds[dev_index] + own_slots, D_NEW - 1)
    grad_route = routing(
        source_owner,
        source_map - old_bounds[dev_index],
        old_cap,
        pair_cap,
        dev_index,
        dest_owner,
        new_bounds,
        positions,
        wanted,
        own_slots,
        dp_count,
    )
    moment_route = routing(
        source_owner,
        source_map - old_bounds[dev_index],
        old_cap,
        pair_cap,
        dev_index,
        dest_owner,
        new_bounds,
        positions,
        wanted,
        own_slots,
        dp_count,
    )
    stream = hidden_old.astype(jnp.float32)
    squares = jnp.sum(stream * stream * copies, axis=1)
    inv_rms = lax.rsqrt(squares / D_NEW + 1e-05)
    normed = (stream * inv_rms[:, None] * gain_old).astype(jnp.bfloat16)
    normed_slots = jnp.take(normed, slot_unit, axis=1)
    hidden_slots = jnp.take(hidden_old, slot_unit, axis=1)
    weight_block = lax.all_gather(weight_old, "dp", axis=0, tiled=True)
    masked_block = jnp.where(weight_live[:, None], weight_block, jnp.zeros((), weight_block.dtype))
    columns = normed_slots
    key_sums = jnp.dot(columns, masked_block, preferred_element_type=jnp.float32)
    slopes = lax.dot_general(
        cotangent, masked_block, (((1,), (1,)), ((), ())), preferred_element_type=jnp.float32
    )
    scaled = hidden_slots.astype(jnp.float32) * inv_rms[:, None]
    column_terms = jnp.sum(slopes * scaled, axis=0)
    key_sums, column_terms = (key_sums, column_terms)
    projected = key_sums.astype(jnp.bfloat16)
    columns = normed_slots
    grad_own = lax.psum_scatter(
        lax.dot_general(
            columns, cotangent, (((0,), (0,)), ((), ())), preferred_element_type=jnp.float32
        ),
        "dp",
        scatter_dimension=0,
        tiled=True,
    )
    grad_own = lax.psum(grad_own.astype(jnp.bfloat16), "rep").astype(jnp.float32)
    column_total = lax.psum(column_terms, ("dp", "rep"))
    gain_grad = jnp.where(keep_mask, column_total[source_slot], 0.0)
    moved_grad, moved_first, moved_second = (
        lax.all_to_all(
            outgoing(grad_own, grad_route), "dp", split_axis=0, concat_axis=0, tiled=True
        ),
        lax.all_to_all(
            outgoing(moment_first, moment_route), "dp", split_axis=0, concat_axis=0, tiled=True
        ),
        lax.all_to_all(
            outgoing(moment_second, moment_route), "dp", split_axis=0, concat_axis=0, tiled=True
        ),
    )
    grad_new = arrived(moved_grad, grad_route, live_new)
    first_next = jnp.where(
        live_new[:, None], 0.9 * arrived(moved_first, moment_route, live_new) + 0.1 * grad_new, 0.0
    )
    second_next = jnp.where(
        live_new[:, None],
        0.95 * arrived(moved_second, moment_route, live_new) + 0.05 * grad_new * grad_new,
        0.0,
    )
    adam_step = first_next / (jnp.sqrt(second_next) + 1e-08)
    return (projected, gain_grad, first_next, second_next, adam_step)


def solution(mesh):
    placed = (
        P(("dp", "rep"), None),
        P(("dp", "rep"), None),
        P(),
        P(),
        P(),
        P(),
        P("dp", None),
        P("dp", None),
        P("dp", None),
    )
    return jax.shard_map(
        on_device,
        mesh=mesh,
        in_specs=placed,
        out_specs=(P(("dp", "rep"), None), P(), P("dp", None), P("dp", None), P("dp", None)),
        check_vma=False,
    )
```

profile of v0, /device:TPU:0, one launch (start us, length us, event | category | flops | bytes accessed | tf_op | source)
XLA Modules:
  0.0 749.6 jit_solution(12491640202311818620)
XLA Ops:
  7.8 2.0 fusion.43
  9.9 4.5 compare_select_fusion.25
  14.4 6.3 compare_and_fusion
  20.7 3.2 copy.20
  23.9 1.3 broadcast_subtract_fusion
  25.8 44.6 %scatter_custom_fusion = f32[6144]{0:T(1024)} fusion(s32[8192]{0:T(1024)} %get-tuple-element.42, f32[8192]{0:T(1024)} %broadcast.609, f32[]{:T(128)} %constant.37.clone.1), kind=kCustom, calls=%fused_computation.165 | custom fusion | flops 8192 | bytes 25088 | tf_op jit(solution)/shard_map/scatter-add | solution.py:72
  70.5 1.7 fusion.2
  72.2 2.9 fusion.4
  75.0 33.2 %gather_fusion.12 = bf16[8192,256]{1,0:T(8,128)(2,1)} fusion(bf16[256,6144]{0,1:T(8,128)(2,1)} %fusion.4, s32[8192]{0:T(1024)S(1)} %broadcast_clamp_fusion.3), kind=kCustom, calls=%fused_computation.clone | custom fusion | bytes 8421376 | tf_op jit(solution)/shard_map/jit(_take)/gather | solution.py:115
  108.2 7.2 fusion.5
  115.5 98.0 %reduce-scatter.2.cloned.1.call-done = f32[512,128]{1,0:T(8,128)} async-done(((f32[8192,128]{1,0:T(8,128)}), f32[512,128]{1,0:T(8,128)}) %reduce-scatter.2.cloned.1.call-update) | async-done | bytes 262160 | tf_op jit(solution)/shard_map/reduce_scatter | solution.py:129
  213.5 1.6 convert_element_type.58
  218.0 4.5 compare_select_fusion.7
  222.6 1.0 compare_reduce_fusion.9
  223.5 6.2 select_select_fusion
  231.9 1.0 reduce-window.9
  233.7 1.4 reduce-window.12
  236.0 1.5 convert_subtract_fusion
  237.4 80.7 %gather_fusion.3 = s32[8192]{0:T(1024)} fusion(s32[8192]{0:T(1024)S(1)} %get-tuple-element.31, s32[8192]{0:T(1024)} %broadcast_clamp_fusion), kind=kCustom, calls=%fused_computation.5 | custom fusion | bytes 98304 | tf_op jit(solution)/shard_map/gather | solution.py:29
  318.1 6.1 compare_select_fusion.13
  324.2 30.8 %scatter_custom_fusion.3 = s32[640]{0:T(1024)S(1)} fusion(s32[8192]{0:T(1024)} %bitcast.97, s32[8192]{0:T(1024)S(1)} %iota.49, s32[]{:T(128)} %constant.38.clone.1), kind=kCustom, calls=%fused_computation.178 | custom fusion | bytes 3072 | tf_op jit(solution)/shard_map/scatter | solution.py:31
  355.1 3.9 gather_fusion.4
  359.0 2.3 gather_fusion.5
  361.2 3.2 gather_fusion.10
  364.5 34.7 %scatter_custom_fusion.2 = pred[640]{0:T(1024)(128)(4,1)S(1)} fusion(s32[8192]{0:T(1024)} %bitcast.98, pred[8192]{0:T(1024)(128)(4,1)S(1)} %broadcast.610, pred[]{:T(512)} %constant.95.clone.1), kind=kCustom, calls=%fused_computation.180 | custom fusion | bytes 1152 | tf_op jit(solution)/shard_map/scatter | solution.py:32
  400.6 3.9 gather_fusion.6
  406.4 44.3 %scatter_custom_fusion.1 = s32[6144]{0:T(1024)S(1)} fusion(s32[8192]{0:T(1024)} %get-tuple-element.42, s32[8192]{0:T(1024)} %iota.45, s32[]{:T(128)} %constant.34.clone.1), kind=kCustom, calls=%fused_computation.163 | custom fusion | flops 8192 | bytes 25088 | tf_op jit(solution)/shard_map/scatter-min | solution.py:69
  458.2 1.6 convert_element_type.59
  459.8 3.2 gather_fusion.8
  463.0 2.3 broadcast_select_fusion.8
  465.2 5.2 all-to-all-start.2
  471.1 32.9 %gather_fusion.13 = bf16[8192,256]{1,0:T(8,128)(2,1)} fusion(bf16[256,6144]{0,1:T(8,128)(2,1)S(1)} %copy.20, s32[8192]{0:T(1024)S(1)} %copy-done.6), kind=kCustom, calls=%fused_computation.1.clone | custom fusion | bytes 8421376 | tf_op jit(solution)/shard_map/jit(_take)/gather | solution.py:116
  504.1 6.4 copy.22
  510.5 45.5 %gather_fusion.1 = s32[8192]{0:T(1024)S(1)} fusion(s32[6144]{0:T(1024)S(1)} %scatter_custom_fusion.1, s32[8192]{0:T(1024)S(1)} %copy-done.13), kind=kCustom, calls=%fused_computation.3 | custom fusion | bytes 98304 | tf_op jit(solution)/shard_map/gather | solution.py:71
  556.2 50.7 %gather_fusion = pred[8192]{0:T(1024)(128)(4,1)S(1)} fusion(pred[6144]{0:T(1024)(128)(4,1)S(1)} %broadcast_compare_fusion.1, s32[8192]{0:T(1024)S(1)} %copy-done.9), kind=kCustom, calls=%fused_computation.2 | custom fusion | bytes 49152 | tf_op jit(solution)/shard_map/gather | solution.py:78
  606.9 1.0 compare_reduce_fusion.19
  608.0 6.3 fusion.25
  614.3 6.3 fusion.22
  620.7 6.9 all-to-all-start
  627.6 7.3 fusion.9
  635.0 40.8 %psum.14 = f32[8192]{0:T(1024)S(1)} all-reduce(f32[8192]{0:T(1024)S(1)} %fusion.9), channel_id=1, replica_groups=mesh['dp'=16,'rep'=2] {'dp','rep'}, use_global_device_ids=true, to_apply=%region_4.6 | all-reduce | flops 8192 | bytes 65536 | tf_op jit(solution)/shard_map/psum | solution.py:138
  675.8 45.5 %gather_fusion.2 = f32[8192]{0:T(1024)S(1)} fusion(f32[8192]{0:T(1024)S(1)} %psum.14, s32[8192]{0:T(1024)S(1)} %fusion.22), kind=kCustom, calls=%fused_computation.4 | custom fusion | bytes 98304 | tf_op jit(solution)/shard_map/gather | solution.py:139
  721.4 5.4 all-to-all-start.1
  727.4 8.4 %fusion.11 = bf16[256,128]{1,0:T(8,128)(2,1)} fusion(bf16[8192,256]{1,0:T(8,128)(2,1)} %gather_fusion.12, pred[8192]{0:T(1024)(128)(4,1)S(1)} %get-tuple-element.37, bf16[8192,128]{1,0:T(8,128)(2,1)S(1)} %copy-done.28, pred[8192]{0:T(1024)(128)(4,1)S(1)} %fusion.25), kind=kOutput, calls=%fused_computation.36 | convolution fusion | flops 540049408 | bytes 6373376 | tf_op jit(solution)/shard_map/dot_general | solution.py:120
  735.8 2.6 gather_fusion.11
  738.4 1.7 gather_fusion.7
  740.1 1.7 gather_fusion.9
  741.8 1.2 add_divide_fusion
  (123 shorter events, 18.8 us)
Async XLA Ops:
  7.2 351.8 %copy-start = (f32[512,128]{1,0:T(8,128)S(1)}, f32[512,128]{1,0:T(8,128)}, u32[]{:S(2)}) copy-start(f32[512,128]{1,0:T(8,128)} %param.18) | copy-start | bytes 786436
  7.2 16.8 %copy-start.2 = (s32[8192]{0:T(1024)S(1)}, s32[8192]{0:T(1024)}, u32[]{:S(2)}) copy-start(s32[8192]{0:T(1024)} %param.16) | copy-start | bytes 98308
  7.2 206.3 %reduce-scatter.2.cloned.1.call-start = ((), (), s32[]{:S(2)}) async-start(), calls=%async_computation.5 | async-start | bytes 4456448 | tf_op jit(solution)/shard_map/reduce_scatter | solution.py:129
  20.7 54.3 %copy-start.5 = (s32[8192]{0:T(1024)}, s32[8192]{0:T(1024)S(1)}, u32[]{:S(2)}) copy-start(s32[8192]{0:T(1024)S(1)} %broadcast_clamp_fusion.3) | copy-start | bytes 98308
  72.2 36.1 %copy-start.25 = (f32[256]{0:T(256)}, f32[256]{0:T(256)S(1)}, u32[]{:S(2)}) copy-start(f32[256]{0:T(256)S(1)} %add_rsqrt_fusion) | copy-start | bytes 3076
  115.4 100.4 %copy-start.8 = (s32[17]{0:T(128)S(1)}, s32[17]{0:T(128)}, u32[]{:S(2)}) copy-start(s32[17]{0:T(128)} %param.15) | copy-start | bytes 208
  115.4 101.1 %copy-start.7 = (s32[17]{0:T(128)S(1)}, s32[17]{0:T(128)}, u32[]{:S(2)}) copy-start(s32[17]{0:T(128)} %param.14) | copy-start | bytes 208
  115.4 342.7 %all-reduce.2.cloned.1.call-start = ((), (), s32[]{:S(2)}) async-start(), calls=%async_computation.6 | async-start | bytes 262144 | tf_op jit(solution)/shard_map/psum | solution.py:137
  215.1 412.5 %all-gather.2.cloned.1.call-start = ((), (), s32[]{:S(2)}) async-start(), calls=%async_computation.4 | async-start | bytes 2228224 | tf_op jit(solution)/shard_map/all_gather | solution.py:117
  218.0 11.8 %copy-start.4 = (s32[8192]{0:T(1024)}, s32[8192]{0:T(1024)S(1)}, u32[]{:S(2)}) copy-start(s32[8192]{0:T(1024)S(1)} %convert_reduce_fusion.1) | copy-start | bytes 98308
  233.0 3.0 copy-start.1
  404.4 66.7 %copy-start.6 = (s32[8192]{0:T(1024)S(1)}, s32[8192]{0:T(1024)}, u32[]{:S(2)}) copy-start(s32[8192]{0:T(1024)} %copy-done.5) | copy-start | bytes 98308
  465.2 155.4 %all-to-all-start.2 = ((f32[16,40,128]{2,1,0:T(8,128)}), f32[16,40,128]{2,1,0:T(8,128)}, u32[]{:S(2)}, u32[]{:S(2)}) async-start(f32[16,40,128]{2,1,0:T(8,128)} %get-tuple-element.45), calls=%async_computation.3 | async-start | bytes 655360 | tf_op jit(solution)/shard_map/all_to_all | solution.py:147
  504.1 6.4 copy-start.13
  510.4 45.5 %copy-start.9 = (s32[8192]{0:T(1024)S(1)}, s32[8192]{0:T(1024)}, u32[]{:S(2)}) copy-start(s32[8192]{0:T(1024)} %broadcast_clamp_fusion.2) | copy-start | bytes 98308
  556.0 50.9 %copy-start.10 = (s32[8192,1]{0,1:T(1,128)S(1)}, s32[8192,1]{0,1:T(1,128)}, u32[]{:S(2)}) copy-start(s32[8192,1]{0,1:T(1,128)} %get-tuple-element.36) | copy-start | bytes 98308
  556.0 51.9 %copy-start.12 = (s32[8192,1]{0,1:T(1,128)S(1)}, s32[8192,1]{0,1:T(1,128)}, u32[]{:S(2)}) copy-start(s32[8192,1]{0,1:T(1,128)} %get-tuple-element.82) | copy-start | bytes 98308
  556.0 51.9 %copy-start.15 = (pred[8192]{0:T(1024)(128)(4,1)S(1)}, pred[8192]{0:T(1024)(128)(4,1)}, u32[]{:S(2)}) copy-start(pred[8192]{0:T(1024)(128)(4,1)} %compare_reduce_fusion.20) | copy-start | bytes 24580
  556.0 51.9 %copy-start.16 = (pred[8192]{0:T(1024)(128)(4,1)S(1)}, pred[8192]{0:T(1024)(128)(4,1)}, u32[]{:S(2)}) copy-start(pred[8192]{0:T(1024)(128)(4,1)} %compare_reduce_fusion.21) | copy-start | bytes 24580
  556.0 51.9 %copy-start.17 = (pred[8192]{0:T(1024)(128)(4,1)S(1)}, pred[8192]{0:T(1024)(128)(4,1)}, u32[]{:S(2)}) copy-start(pred[8192]{0:T(1024)(128)(4,1)} %compare_reduce_fusion.22) | copy-start | bytes 24580
  556.0 51.9 %copy-start.18 = (pred[8192]{0:T(1024)(128)(4,1)S(1)}, pred[8192]{0:T(1024)(128)(4,1)}, u32[]{:S(2)}) copy-start(pred[8192]{0:T(1024)(128)(4,1)} %compare_reduce_fusion.23) | copy-start | bytes 24580
  556.1 51.9 %copy-start.19 = (pred[8192]{0:T(1024)(128)(4,1)S(1)}, pred[8192]{0:T(1024)(128)(4,1)}, u32[]{:S(2)}) copy-start(pred[8192]{0:T(1024)(128)(4,1)} %compare_reduce_fusion.24) | copy-start | bytes 24580
  556.1 51.9 %copy-start.20 = (pred[8192]{0:T(1024)(128)(4,1)S(1)}, pred[8192]{0:T(1024)(128)(4,1)}, u32[]{:S(2)}) copy-start(pred[8192]{0:T(1024)(128)(4,1)} %compare_reduce_fusion.25) | copy-start | bytes 24580
  556.1 51.9 %copy-start.21 = (pred[8192]{0:T(1024)(128)(4,1)S(1)}, pred[8192]{0:T(1024)(128)(4,1)}, u32[]{:S(2)}) copy-start(pred[8192]{0:T(1024)(128)(4,1)} %compare_reduce_fusion.26) | copy-start | bytes 24580
  556.1 51.9 %copy-start.22 = (pred[8192]{0:T(1024)(128)(4,1)S(1)}, pred[8192]{0:T(1024)(128)(4,1)}, u32[]{:S(2)}) copy-start(pred[8192]{0:T(1024)(128)(4,1)} %compare_reduce_fusion.27) | copy-start | bytes 24580
  556.1 51.9 %copy-start.23 = (pred[8192]{0:T(1024)(128)(4,1)S(1)}, pred[8192]{0:T(1024)(128)(4,1)}, u32[]{:S(2)}) copy-start(pred[8192]{0:T(1024)(128)(4,1)} %compare_reduce_fusion.28) | copy-start | bytes 24580
  556.1 51.9 %copy-start.24 = (pred[8192]{0:T(1024)(128)(4,1)S(1)}, pred[8192]{0:T(1024)(128)(4,1)}, u32[]{:S(2)}) copy-start(pred[8192]{0:T(1024)(128)(4,1)} %compare_reduce_fusion.29) | copy-start | bytes 24580
  556.1 58.2 %copy-start.3 = (s32[8192]{0:T(1024)S(1)}, s32[8192]{0:T(1024)}, u32[]{:S(2)}) copy-start(s32[8192]{0:T(1024)} %param.16) | copy-start | bytes 98308
  556.1 58.2 %copy-start.11 = (s32[8192,1]{0,1:T(1,128)S(1)}, s32[8192,1]{0,1:T(1,128)}, u32[]{:S(2)}) copy-start(s32[8192,1]{0,1:T(1,128)} %get-tuple-element.35) | copy-start | bytes 98308
  556.1 71.5 %copy-start.14 = (bf16[256,128]{1,0:T(8,128)(2,1)S(1)}, bf16[256,128]{1,0:T(8,128)(2,1)}, u32[]{:S(2)}) copy-start(bf16[256,128]{1,0:T(8,128)(2,1)} %param.12) | copy-start | bytes 196612
  556.1 71.5 %copy-start.26 = (f32[256]{0:T(256)S(1)}, f32[256]{0:T(256)}, u32[]{:S(2)}) copy-start(f32[256]{0:T(256)} %copy-done.25) | copy-start | bytes 3076
  620.7 100.7 %all-to-all-start = ((f32[16,40,128]{2,1,0:T(8,128)}), f32[16,40,128]{2,1,0:T(8,128)S(1)}, u32[]{:S(2)}, u32[]{:S(2)}) async-start(f32[16,40,128]{2,1,0:T(8,128)} %get-tuple-element.43), calls=%async_computation | async-start | bytes 655360 | tf_op jit(solution)/shard_map/all_to_all | solution.py:144
  675.8 51.6 %copy-start.28 = (bf16[8192,128]{1,0:T(8,128)(2,1)S(1)}, bf16[8192,128]{1,0:T(8,128)(2,1)}, u32[]{:S(2)}) copy-start(bf16[8192,128]{1,0:T(8,128)(2,1)} %all-gather.2.cloned.1.call-done) | copy-start | bytes 6291460
  721.4 18.7 %all-to-all-start.1 = ((f32[16,40,128]{2,1,0:T(8,128)}), f32[16,40,128]{2,1,0:T(8,128)S(1)}, u32[]{:S(2)}, u32[]{:S(2)}) async-start(f32[16,40,128]{2,1,0:T(8,128)} %get-tuple-element.44), calls=%async_computation.2 | async-start | bytes 655360 | tf_op jit(solution)/shard_map/all_to_all | solution.py:141
  735.8 6.0 copy-start.27
Sparse Core Ops, SparseCore 0:
  115.6 97.8 reduce-scatter.1
  216.3 17.4 all-reduce.1
  236.6 61.8 all-gather.1
where the time goes:
time: 752 us; the launch traced here: 750 us
  local copies, waits for them, and re-layouts  394 us (52%)
  other arithmetic  160 us (21%)
  waiting for transfers between devices  98.7 us (13%)
  blocking collectives  40.8 us (5%)
  matrix products  22.9 us (3%)
  starting transfers between devices  17.7 us (2%)
  between operations  15.8 us (2%)
    reduce_scatter x1, waiting for transfers between devices, on_device(): lax.psum_scatter(lax.dot_general(columns, cotangent, (((0,), (0,)), ((),...  98 us
    gather x2, local copies, waits for them, and re-layouts, routing(): send_slot = before - before[new_bounds[dest_owner]]  81.3 us
    gather x1, local copies, waits for them, and re-layouts, on_device(): weight_live = live_old & unit_used[slot_unit]  50.7 us
    gather x1, local copies, waits for them, and re-layouts, on_device(): gain_grad = jnp.where(keep_mask, column_total[source_slot], 0.0)  45.5 us
    gather x1, local copies, waits for them, and re-layouts, on_device(): keep_mask = first_use[source_map] == positions  45.5 us
    scatter-add x1, other arithmetic, on_device(): copies = jnp.zeros((D_OLD,), jnp.float32).at[source_map].add(1.0)  44.6 us
    another operation x1, other arithmetic, on_device(): jnp.full((D_OLD,), D_NEW, jnp.int32).at[source_map].min(positions)  44.3 us
    psum x1, blocking collectives, on_device(): column_total = lax.psum(column_terms, ('dp', 'rep'))  40.8 us
  transfers between devices with their start and end apart: 6, of which 1 were waited for; matrix products, arithmetic and copies ran while one was open for 62% of the time, Pallas kernels for 0%

commit v1 on v0

--- a/solution.py
+++ b/solution.py
@@ -59,6 +59,12 @@
     moment_first,
     moment_second,
 ):
+
+    def mix_halves(buf, chip_axis, axis_key):
+        for ii in (chip_axis, axis_key):
+            buf = lax.psum(buf, axis_name=ii)
+        return buf
+
     dp_count = lax.axis_size("dp")
     dev_index = lax.axis_index("dp")
     old_cap = weight_old.shape[0]
@@ -135,7 +141,7 @@
         tiled=True,
     )
     grad_own = lax.psum(grad_own.astype(jnp.bfloat16), "rep").astype(jnp.float32)
-    column_total = lax.psum(column_terms, ("dp", "rep"))
+    column_total = mix_halves(column_terms, "rep", "dp")
     gain_grad = jnp.where(keep_mask, column_total[source_slot], 0.0)
     moved_grad, moved_first, moved_second = (
         lax.all_to_all(

time: 752 us -> 790 us (1.051)
  blocking collectives: 40.8 us -> 80.5 us
    psum x1 -> x2, blocking collectives: 40.8 us -> 80.5 us  [mix_halves(): buf = lax.psum(buf, axis_name=ii)]
  transfers between devices with their start and end apart: 6 -> 6, of which waited for: 1 -> 1; matrix products, arithmetic and copies ran while one was open for 62% -> 59% of each run, Pallas kernels for 0% -> 0%
where the time goes in v1:
time: 790 us; the launch traced here: 787 us
  local copies, waits for them, and re-layouts  394 us (50%)
  other arithmetic  160 us (20%)
  waiting for transfers between devices  98.7 us (12%)
  blocking collectives  80.5 us (10%)
  matrix products  22.9 us (3%)
  starting transfers between devices  15.8 us (2%)
  between operations  15.8 us (2%)
    reduce_scatter x1, waiting for transfers between devices, on_device(): lax.psum_scatter(lax.dot_general(columns, cotangent, (((0,), (0,)), ((),...  98 us
    gather x2, local copies, waits for them, and re-layouts, routing(): send_slot = before - before[new_bounds[dest_owner]]  81.3 us
    psum x2, blocking collectives, mix_halves(): buf = lax.psum(buf, axis_name=ii)  80.5 us
    gather x1, local copies, waits for them, and re-layouts, on_device(): weight_live = live_old & unit_used[slot_unit]  50.7 us
    gather x1, local copies, waits for them, and re-layouts, on_device(): keep_mask = first_use[source_map] == positions  45.5 us
    gather x1, local copies, waits for them, and re-layouts, on_device(): gain_grad = jnp.where(keep_mask, column_total[source_slot], 0.0)  45.5 us
    scatter-add x1, other arithmetic, on_device(): copies = jnp.zeros((D_OLD,), jnp.float32).at[source_map].add(1.0)  44.6 us
    another operation x1, other arithmetic, on_device(): jnp.full((D_OLD,), D_NEW, jnp.int32).at[source_map].min(positions)  44.3 us
  transfers between devices with their start and end apart: 6, of which 1 were waited for; matrix products, arithmetic and copies ran while one was open for 59% of the time, Pallas kernels for 0%

profile of v1, /device:TPU:0, one launch (start us, length us, event | category | flops | bytes accessed | tf_op | source)
XLA Modules:
  0.0 787.4 jit_solution(10755453295044611267)
XLA Ops:
  7.8 2.0 fusion.43
  9.9 4.5 compare_select_fusion.25
  14.4 6.3 compare_and_fusion
  20.7 3.2 copy.20
  23.9 1.3 broadcast_subtract_fusion
  25.8 44.6 %scatter_custom_fusion = f32[6144]{0:T(1024)} fusion(s32[8192]{0:T(1024)} %get-tuple-element.42, f32[8192]{0:T(1024)} %broadcast.609, f32[]{:T(128)} %constant.37.clone.1), kind=kCustom, calls=%fused_computation.165 | custom fusion | flops 8192 | bytes 25088 | tf_op jit(solution)/shard_map/scatter-add | solution.py:78
  70.5 1.7 fusion.2
  72.2 2.9 fusion.4
  75.0 33.2 %gather_fusion.12 = bf16[8192,256]{1,0:T(8,128)(2,1)} fusion(bf16[256,6144]{0,1:T(8,128)(2,1)} %fusion.4, s32[8192]{0:T(1024)S(1)} %broadcast_clamp_fusion.3), kind=kCustom, calls=%fused_computation.clone | custom fusion | bytes 8421376 | tf_op jit(solution)/shard_map/jit(_take)/gather | solution.py:121
  108.2 7.2 fusion.5
  115.5 98.0 %reduce-scatter.2.cloned.1.call-done = f32[512,128]{1,0:T(8,128)} async-done(((f32[8192,128]{1,0:T(8,128)}), f32[512,128]{1,0:T(8,128)}) %reduce-scatter.2.cloned.1.call-update) | async-done | bytes 262160 | tf_op jit(solution)/shard_map/reduce_scatter | solution.py:135
  213.5 1.6 convert_element_type.58
  218.0 4.5 compare_select_fusion.7
  222.6 1.0 compare_reduce_fusion.9
  223.5 6.2 select_select_fusion
  231.9 1.0 reduce-window.9
  233.7 1.4 reduce-window.12
  236.0 1.5 convert_subtract_fusion
  237.4 80.7 %gather_fusion.3 = s32[8192]{0:T(1024)} fusion(s32[8192]{0:T(1024)S(1)} %get-tuple-element.31, s32[8192]{0:T(1024)} %broadcast_clamp_fusion), kind=kCustom, calls=%fused_computation.5 | custom fusion | bytes 98304 | tf_op jit(solution)/shard_map/gather | solution.py:29
  318.1 6.1 compare_select_fusion.13
  324.2 30.8 %scatter_custom_fusion.3 = s32[640]{0:T(1024)S(1)} fusion(s32[8192]{0:T(1024)} %bitcast.97, s32[8192]{0:T(1024)S(1)} %iota.49, s32[]{:T(128)} %constant.38.clone.1), kind=kCustom, calls=%fused_computation.178 | custom fusion | bytes 3072 | tf_op jit(solution)/shard_map/scatter | solution.py:31
  355.1 3.9 gather_fusion.4
  359.0 2.3 gather_fusion.5
  361.2 3.2 gather_fusion.10
  364.5 34.7 %scatter_custom_fusion.2 = pred[640]{0:T(1024)(128)(4,1)S(1)} fusion(s32[8192]{0:T(1024)} %bitcast.98, pred[8192]{0:T(1024)(128)(4,1)S(1)} %broadcast.610, pred[]{:T(512)} %constant.95.clone.1), kind=kCustom, calls=%fused_computation.180 | custom fusion | bytes 1152 | tf_op jit(solution)/shard_map/scatter | solution.py:32
  400.6 3.9 gather_fusion.6
  406.4 44.3 %scatter_custom_fusion.1 = s32[6144]{0:T(1024)S(1)} fusion(s32[8192]{0:T(1024)} %get-tuple-element.42, s32[8192]{0:T(1024)} %iota.45, s32[]{:T(128)} %constant.34.clone.1), kind=kCustom, calls=%fused_computation.163 | custom fusion | flops 8192 | bytes 25088 | tf_op jit(solution)/shard_map/scatter-min | solution.py:75
  458.2 1.6 convert_element_type.59
  459.8 3.2 gather_fusion.8
  463.0 2.3 broadcast_select_fusion.8
  465.2 5.2 all-to-all-start.2
  471.1 32.9 %gather_fusion.13 = bf16[8192,256]{1,0:T(8,128)(2,1)} fusion(bf16[256,6144]{0,1:T(8,128)(2,1)S(1)} %copy.20, s32[8192]{0:T(1024)S(1)} %copy-done.6), kind=kCustom, calls=%fused_computation.1.clone | custom fusion | bytes 8421376 | tf_op jit(solution)/shard_map/jit(_take)/gather | solution.py:122
  504.1 6.4 copy.22
  510.5 45.5 %gather_fusion.1 = s32[8192]{0:T(1024)S(1)} fusion(s32[6144]{0:T(1024)S(1)} %scatter_custom_fusion.1, s32[8192]{0:T(1024)S(1)} %copy-done.13), kind=kCustom, calls=%fused_computation.3 | custom fusion | bytes 98304 | tf_op jit(solution)/shard_map/gather | solution.py:77
  556.2 50.7 %gather_fusion = pred[8192]{0:T(1024)(128)(4,1)S(1)} fusion(pred[6144]{0:T(1024)(128)(4,1)S(1)} %broadcast_compare_fusion.1, s32[8192]{0:T(1024)S(1)} %copy-done.9), kind=kCustom, calls=%fused_computation.2 | custom fusion | bytes 49152 | tf_op jit(solution)/shard_map/gather | solution.py:84
  608.0 6.3 fusion.25
  614.3 6.3 fusion.22
  620.7 6.9 all-to-all-start
  627.6 7.3 fusion.9
  635.0 3.4 psum.21
  638.4 77.1 %psum.22 = f32[8192]{0:T(1024)S(1)} all-reduce(f32[8192]{0:T(1024)S(1)} %psum.21), channel_id=1, replica_groups=mesh['dp'=16,'rep'=2] {'dp'}, use_global_device_ids=true, to_apply=%region_5.7 | all-reduce | flops 8192 | bytes 65536 | tf_op jit(solution)/shard_map/psum | solution.py:65
  715.5 45.5 %gather_fusion.2 = f32[8192]{0:T(1024)S(1)} fusion(f32[8192]{0:T(1024)S(1)} %psum.22, s32[8192]{0:T(1024)S(1)} %fusion.22), kind=kCustom, calls=%fused_computation.4 | custom fusion | bytes 98304 | tf_op jit(solution)/shard_map/gather | solution.py:145
  761.1 3.6 all-to-all-start.1
  765.3 8.4 %fusion.11 = bf16[256,128]{1,0:T(8,128)(2,1)} fusion(bf16[8192,256]{1,0:T(8,128)(2,1)} %gather_fusion.12, pred[8192]{0:T(1024)(128)(4,1)S(1)} %get-tuple-element.37, bf16[8192,128]{1,0:T(8,128)(2,1)S(1)} %copy-done.28, pred[8192]{0:T(1024)(128)(4,1)S(1)} %fusion.25), kind=kOutput, calls=%fused_computation.36 | convolution fusion | flops 540049408 | bytes 6373376 | tf_op jit(solution)/shard_map/dot_general | solution.py:126
  773.6 2.6 gather_fusion.11
  776.3 1.7 gather_fusion.7
  777.9 1.7 gather_fusion.9
  779.6 1.2 add_divide_fusion
  (124 shorter events, 19.7 us)
Async XLA Ops:
  7.2 351.8 %copy-start = (f32[512,128]{1,0:T(8,128)S(1)}, f32[512,128]{1,0:T(8,128)}, u32[]{:S(2)}) copy-start(f32[512,128]{1,0:T(8,128)} %param.18) | copy-start | bytes 786436
  7.2 16.8 %copy-start.2 = (s32[8192]{0:T(1024)S(1)}, s32[8192]{0:T(1024)}, u32[]{:S(2)}) copy-start(s32[8192]{0:T(1024)} %param.16) | copy-start | bytes 98308
  7.2 206.3 %reduce-scatter.2.cloned.1.call-start = ((), (), s32[]{:S(2)}) async-start(), calls=%async_computation.5 | async-start | bytes 4456448 | tf_op jit(solution)/shard_map/reduce_scatter | solution.py:135
  20.7 54.3 %copy-start.5 = (s32[8192]{0:T(1024)}, s32[8192]{0:T(1024)S(1)}, u32[]{:S(2)}) copy-start(s32[8192]{0:T(1024)S(1)} %broadcast_clamp_fusion.3) | copy-start | bytes 98308
  72.2 36.1 %copy-start.25 = (f32[256]{0:T(256)}, f32[256]{0:T(256)S(1)}, u32[]{:S(2)}) copy-start(f32[256]{0:T(256)S(1)} %add_rsqrt_fusion) | copy-start | bytes 3076
  115.4 100.4 %copy-start.8 = (s32[17]{0:T(128)S(1)}, s32[17]{0:T(128)}, u32[]{:S(2)}) copy-start(s32[17]{0:T(128)} %param.15) | copy-start | bytes 208
  115.4 101.1 %copy-start.7 = (s32[17]{0:T(128)S(1)}, s32[17]{0:T(128)}, u32[]{:S(2)}) copy-start(s32[17]{0:T(128)} %param.14) | copy-start | bytes 208
  115.4 342.7 %all-reduce.2.cloned.1.call-start = ((), (), s32[]{:S(2)}) async-start(), calls=%async_computation.6 | async-start | bytes 262144 | tf_op jit(solution)/shard_map/psum | solution.py:143
  215.1 412.5 %all-gather.2.cloned.1.call-start = ((), (), s32[]{:S(2)}) async-start(), calls=%async_computation.4 | async-start | bytes 2228224 | tf_op jit(solution)/shard_map/all_gather | solution.py:123
  218.0 11.8 %copy-start.4 = (s32[8192]{0:T(1024)}, s32[8192]{0:T(1024)S(1)}, u32[]{:S(2)}) copy-start(s32[8192]{0:T(1024)S(1)} %convert_reduce_fusion.1) | copy-start | bytes 98308
  233.0 3.0 copy-start.1
  404.4 66.7 %copy-start.6 = (s32[8192]{0:T(1024)S(1)}, s32[8192]{0:T(1024)}, u32[]{:S(2)}) copy-start(s32[8192]{0:T(1024)} %copy-done.5) | copy-start | bytes 98308
  465.2 155.4 %all-to-all-start.2 = ((f32[16,40,128]{2,1,0:T(8,128)}), f32[16,40,128]{2,1,0:T(8,128)}, u32[]{:S(2)}, u32[]{:S(2)}) async-start(f32[16,40,128]{2,1,0:T(8,128)} %get-tuple-element.45), calls=%async_computation.3 | async-start | bytes 655360 | tf_op jit(solution)/shard_map/all_to_all | solution.py:153
  504.1 6.4 copy-start.13
  510.4 45.5 %copy-start.9 = (s32[8192]{0:T(1024)S(1)}, s32[8192]{0:T(1024)}, u32[]{:S(2)}) copy-start(s32[8192]{0:T(1024)} %broadcast_clamp_fusion.2) | copy-start | bytes 98308
  556.0 50.9 %copy-start.10 = (s32[8192,1]{0,1:T(1,128)S(1)}, s32[8192,1]{0,1:T(1,128)}, u32[]{:S(2)}) copy-start(s32[8192,1]{0,1:T(1,128)} %get-tuple-element.36) | copy-start | bytes 98308
  556.0 51.9 %copy-start.12 = (s32[8192,1]{0,1:T(1,128)S(1)}, s32[8192,1]{0,1:T(1,128)}, u32[]{:S(2)}) copy-start(s32[8192,1]{0,1:T(1,128)} %get-tuple-element.82) | copy-start | bytes 98308
  556.0 51.9 %copy-start.15 = (pred[8192]{0:T(1024)(128)(4,1)S(1)}, pred[8192]{0:T(1024)(128)(4,1)}, u32[]{:S(2)}) copy-start(pred[8192]{0:T(1024)(128)(4,1)} %compare_reduce_fusion.20) | copy-start | bytes 24580
  556.0 51.9 %copy-start.16 = (pred[8192]{0:T(1024)(128)(4,1)S(1)}, pred[8192]{0:T(1024)(128)(4,1)}, u32[]{:S(2)}) copy-start(pred[8192]{0:T(1024)(128)(4,1)} %compare_reduce_fusion.21) | copy-start | bytes 24580
  556.0 51.9 %copy-start.17 = (pred[8192]{0:T(1024)(128)(4,1)S(1)}, pred[8192]{0:T(1024)(128)(4,1)}, u32[]{:S(2)}) copy-start(pred[8192]{0:T(1024)(128)(4,1)} %compare_reduce_fusion.22) | copy-start | bytes 24580
  556.0 51.9 %copy-start.18 = (pred[8192]{0:T(1024)(128)(4,1)S(1)}, pred[8192]{0:T(1024)(128)(4,1)}, u32[]{:S(2)}) copy-start(pred[8192]{0:T(1024)(128)(4,1)} %compare_reduce_fusion.23) | copy-start | bytes 24580
  556.1 51.9 %copy-start.19 = (pred[8192]{0:T(1024)(128)(4,1)S(1)}, pred[8192]{0:T(1024)(128)(4,1)}, u32[]{:S(2)}) copy-start(pred[8192]{0:T(1024)(128)(4,1)} %compare_reduce_fusion.24) | copy-start | bytes 24580
  556.1 51.9 %copy-start.20 = (pred[8192]{0:T(1024)(128)(4,1)S(1)}, pred[8192]{0:T(1024)(128)(4,1)}, u32[]{:S(2)}) copy-start(pred[8192]{0:T(1024)(128)(4,1)} %compare_reduce_fusion.25) | copy-start | bytes 24580
  556.1 51.9 %copy-start.21 = (pred[8192]{0:T(1024)(128)(4,1)S(1)}, pred[8192]{0:T(1024)(128)(4,1)}, u32[]{:S(2)}) copy-start(pred[8192]{0:T(1024)(128)(4,1)} %compare_reduce_fusion.26) | copy-start | bytes 24580
  556.1 51.9 %copy-start.22 = (pred[8192]{0:T(1024)(128)(4,1)S(1)}, pred[8192]{0:T(1024)(128)(4,1)}, u32[]{:S(2)}) copy-start(pred[8192]{0:T(1024)(128)(4,1)} %compare_reduce_fusion.27) | copy-start | bytes 24580
  556.1 51.9 %copy-start.23 = (pred[8192]{0:T(1024)(128)(4,1)S(1)}, pred[8192]{0:T(1024)(128)(4,1)}, u32[]{:S(2)}) copy-start(pred[8192]{0:T(1024)(128)(4,1)} %compare_reduce_fusion.28) | copy-start | bytes 24580
  556.1 51.9 %copy-start.24 = (pred[8192]{0:T(1024)(128)(4,1)S(1)}, pred[8192]{0:T(1024)(128)(4,1)}, u32[]{:S(2)}) copy-start(pred[8192]{0:T(1024)(128)(4,1)} %compare_reduce_fusion.29) | copy-start | bytes 24580
  556.1 58.2 %copy-start.3 = (s32[8192]{0:T(1024)S(1)}, s32[8192]{0:T(1024)}, u32[]{:S(2)}) copy-start(s32[8192]{0:T(1024)} %param.16) | copy-start | bytes 98308
  556.1 58.2 %copy-start.11 = (s32[8192,1]{0,1:T(1,128)S(1)}, s32[8192,1]{0,1:T(1,128)}, u32[]{:S(2)}) copy-start(s32[8192,1]{0,1:T(1,128)} %get-tuple-element.35) | copy-start | bytes 98308
  556.1 71.5 %copy-start.14 = (bf16[256,128]{1,0:T(8,128)(2,1)S(1)}, bf16[256,128]{1,0:T(8,128)(2,1)}, u32[]{:S(2)}) copy-start(bf16[256,128]{1,0:T(8,128)(2,1)} %param.12) | copy-start | bytes 196612
  556.1 71.5 %copy-start.26 = (f32[256]{0:T(256)S(1)}, f32[256]{0:T(256)}, u32[]{:S(2)}) copy-start(f32[256]{0:T(256)} %copy-done.25) | copy-start | bytes 3076
  620.7 140.4 %all-to-all-start = ((f32[16,40,128]{2,1,0:T(8,128)}), f32[16,40,128]{2,1,0:T(8,128)S(1)}, u32[]{:S(2)}, u32[]{:S(2)}) async-start(f32[16,40,128]{2,1,0:T(8,128)} %get-tuple-element.43), calls=%async_computation | async-start | bytes 655360 | tf_op jit(solution)/shard_map/all_to_all | solution.py:150
  715.5 49.7 %copy-start.28 = (bf16[8192,128]{1,0:T(8,128)(2,1)S(1)}, bf16[8192,128]{1,0:T(8,128)(2,1)}, u32[]{:S(2)}) copy-start(bf16[8192,128]{1,0:T(8,128)(2,1)} %all-gather.2.cloned.1.call-done) | copy-start | bytes 6291460
  761.1 16.9 %all-to-all-start.1 = ((f32[16,40,128]{2,1,0:T(8,128)}), f32[16,40,128]{2,1,0:T(8,128)S(1)}, u32[]{:S(2)}, u32[]{:S(2)}) async-start(f32[16,40,128]{2,1,0:T(8,128)} %get-tuple-element.44), calls=%async_computation.2 | async-start | bytes 655360 | tf_op jit(solution)/shard_map/all_to_all | solution.py:147
  773.6 6.0 copy-start.27
Sparse Core Ops, SparseCore 0:
  115.6 97.8 reduce-scatter.1
  216.3 17.4 all-reduce.1
  236.6 61.8 all-gather.1
